TPU v7x, 256 devices: a whole 4x4x8 slice. The times are simulated.
256 devices in a mesh: frame: 16 (over x_hi, z), head: 8 (over y, core), dp: 2 (over x_lo).
Axes of the slice: x: 4 (x_hi: 2, x_lo: 2; x = x_hi * 2 + x_lo), y: 4, z: 8, core: 2. Of those that a mesh axis runs over, the one named last changes fastest.
Arguments:
- clip: bfloat16 [2, 4096, 256], P('dp', 'frame'), may hold values from -40 to 40
- block_ids: int32 [2, 4096], P('dp'), may hold values from 0 to 63, never falling along the last dimension, each value on 1 to 128 neighbouring positions
- w_spatial: bfloat16 [9, 256, 256], replicated, may hold values from -0.125 to 0.125
- w_temporal: bfloat16 [3, 256, 256], replicated, may hold values from -0.21875 to 0.21875
- w_query: bfloat16 [256, 2048], P(None, 'head'), may hold values from -0.375 to 0.375
- w_key: bfloat16 [256, 2048], P(None, 'head'), may hold values from -0.375 to 0.375
- w_value: bfloat16 [256, 2048], P(None, 'head'), may hold values from -0.375 to 0.375
- w_out: bfloat16 [2048, 256], P('head'), may hold values from -0.125 to 0.125
- cotangent: bfloat16 [2, 4096, 256], P('dp', 'frame'), may hold values from -6 to 6
Outputs:
- grad_spatial: float32 [9, 256, 256], replicated
- grad_temporal: float32 [3, 256, 256], replicated
- grad_query: float32 [256, 2048], P(None, 'head')
- grad_key: float32 [256, 2048], P(None, 'head')
- grad_value: float32 [256, 2048], P(None, 'head')
- grad_out: float32 [2048, 256], P('head')
Inputs may be any that keep to these rules, and one draw needn't show every extreme that they name: `block_ids`: block numbers never fall along a clip's tokens; every block has 1 to (128) tokens.
All inputs are finite; a program needn't handle non-finite values.
Results may differ from a plain program's by a relative error of at most 0.04.
Values may be sent and summed in bfloat16 or wider, within the bound.
No kernel may reach another device: no remote copies, remote signals or barrier semaphores. Data moves between devices by JAX's collectives and lax.ppermute only.
A program may use at most 128 MiB of HBM per device.

v0:
```python
import jax
import jax.numpy as jnp
from jax import lax
from jax.sharding import PartitionSpec as P

HD = 128
SIDE = 8
NEG_FILL = -1e30


def with_halo(cells, sides, width):
    for axis, dim in sides:
        count = lax.axis_size(axis)
        ends = count - 1
        head = lax.slice_in_dim(cells, 0, width, axis=dim)
        tail = lax.slice_in_dim(cells, cells.shape[dim] - width, cells.shape[dim], axis=dim)
        cells = jnp.concatenate(
            [
                lax.ppermute(tail, axis, [(i, (i + 1) % count) for i in range(ends)]),
                cells,
                lax.ppermute(head, axis, [((i + 1) % count, i) for i in range(ends)]),
            ],
            axis=dim,
        )
    return cells


def spatial_taps(frame_grid, side):
    padded = jnp.pad(frame_grid, ((0, 0), (1, 1), (1, 1), (0, 0)))
    count = frame_grid.shape[0] * side * side
    width = frame_grid.shape[3]
    return [
        padded[:, row_off : row_off + side, col_off : col_off + side, :].reshape(count, width)
        for row_off in range(3)
        for col_off in range(3)
    ]


def silu_slope(pre_act):
    sigma = jax.nn.sigmoid(pre_act)
    return sigma * (1.0 + pre_act * (1.0 - sigma))


def frame_rims(field):
    return with_halo(field, (("frame", 0),), SIDE * SIDE)


def take_head(matrix, which_head):
    return matrix[:, which_head * HD : (which_head + 1) * HD]


def contract_rows(left, right):
    return lax.dot_general(
        left, right, (((0,), (0,)), ((), ())), preferred_element_type=jnp.float32
    )


def on_device(clip, block_ids, w_spatial, w_temporal, w_query, w_key, w_value, w_out, cotangent):
    frames_in = clip[0]
    upstream = cotangent[0]
    clip_blocks = block_ids[0]
    tok_local, channels = frames_in.shape
    frame_len = SIDE * SIDE
    scale = HD ** (-0.5)
    grid = frames_in.reshape(tok_local // frame_len, SIDE, SIDE, channels)
    taps = spatial_taps(grid, SIDE)
    pre_act = jnp.zeros((tok_local, channels), jnp.float32)
    for offset in range(9):
        pre_act = pre_act + jnp.dot(
            taps[offset], w_spatial[offset], preferred_element_type=jnp.float32
        )
    hidden = jax.nn.silu(pre_act).astype(jnp.bfloat16)
    hidden_rim = frame_rims(hidden)
    temporal = jnp.zeros((tok_local, channels), jnp.float32)
    for offset in range(3):
        temporal = temporal + jnp.dot(
            hidden_rim[offset * frame_len : offset * frame_len + tok_local],
            w_temporal[offset],
            preferred_element_type=jnp.float32,
        )
    features = temporal.astype(jnp.bfloat16)
    queries_local = jnp.dot(features, w_query, preferred_element_type=jnp.float32).astype(
        jnp.bfloat16
    )
    keys_local = jnp.dot(features, w_key, preferred_element_type=jnp.float32).astype(jnp.bfloat16)
    values_local = jnp.dot(features, w_value, preferred_element_type=jnp.float32).astype(
        jnp.bfloat16
    )
    keys_every, values_every = (
        lax.all_gather(keys_local, "frame", axis=0, tiled=True),
        lax.all_gather(values_local, "frame", axis=0, tiled=True),
    )
    first_row = lax.axis_index("frame") * tok_local
    grad_attended = jnp.dot(upstream, w_out.T, preferred_element_type=jnp.float32).astype(
        jnp.bfloat16
    )
    queries_held, grad_held = (queries_local, grad_attended)
    held_blocks = lax.dynamic_slice_in_dim(clip_blocks, first_row, tok_local)
    visible = clip_blocks[None, :] <= held_blocks[:, None]
    heads_here = queries_local.shape[1] // HD
    width_here = queries_local.shape[1]
    attended_parts, grad_query_parts, prob_list, score_grads, norm_list, delta_list = (
        [],
        [],
        [],
        [],
        [],
        [],
    )
    for which_head in range(heads_here):
        query_head = take_head(queries_held, which_head)
        key_head = take_head(keys_every, which_head)
        value_head = take_head(values_every, which_head)
        grad_head = take_head(grad_held, which_head)
        scores = jnp.dot(query_head, key_head.T, preferred_element_type=jnp.float32) * scale
        masked = jnp.where(visible, scores, NEG_FILL)
        top = jnp.max(masked, axis=1, keepdims=True)
        total = jnp.sum(jnp.where(visible, jnp.exp(masked - top), 0.0), axis=1, keepdims=True)
        log_norm = top + jnp.log(total)
        probs = jnp.where(visible, jnp.exp(masked - log_norm), 0.0)
        probs_low = probs.astype(jnp.bfloat16)
        attended = jnp.dot(probs_low, value_head, preferred_element_type=jnp.float32).astype(
            jnp.bfloat16
        )
        delta = jnp.sum(
            grad_head.astype(jnp.float32) * attended.astype(jnp.float32), axis=1, keepdims=True
        )
        grad_probs = jnp.dot(grad_head, value_head.T, preferred_element_type=jnp.float32)
        grad_scores = (probs * (grad_probs - delta) * scale).astype(jnp.bfloat16)
        grad_query_parts.append(
            jnp.dot(grad_scores, key_head, preferred_element_type=jnp.float32).astype(jnp.bfloat16)
        )
        attended_parts.append(attended)
        prob_list.append(probs_low)
        score_grads.append(grad_scores)
        norm_list.append(log_norm)
        delta_list.append(delta)
    attended_all = jnp.concatenate(attended_parts, axis=1)
    grad_queries = jnp.concatenate(grad_query_parts, axis=1)
    key_parts = []
    value_parts = []
    for which_head in range(heads_here):
        score_cols = score_grads[which_head]
        prob_cols = prob_list[which_head]
        key_parts.append(contract_rows(score_cols, take_head(queries_held, which_head)))
        value_parts.append(contract_rows(prob_cols, take_head(grad_held, which_head)))
    summed = lax.psum_scatter(
        jnp.concatenate(key_parts + value_parts, axis=1), "frame", scatter_dimension=0, tiled=True
    )
    grad_keys = summed[:, :width_here].astype(jnp.bfloat16)
    grad_values = summed[:, width_here:].astype(jnp.bfloat16)
    grad_wq_local = contract_rows(features, grad_queries)
    grad_wk_local = contract_rows(features, grad_keys)
    grad_wv_local = contract_rows(features, grad_values)
    grad_wo_local = contract_rows(attended_all, upstream)
    back_part = jnp.dot(grad_queries, w_query.T, preferred_element_type=jnp.float32)
    back_part = back_part + jnp.dot(grad_keys, w_key.T, preferred_element_type=jnp.float32)
    back_part = back_part + jnp.dot(grad_values, w_value.T, preferred_element_type=jnp.float32)
    head_sum = lax.psum(back_part, "head")
    grad_features = (head_sum + upstream.astype(jnp.float32)).astype(jnp.bfloat16)
    grad_rim = frame_rims(grad_features)
    grad_wt = jnp.stack(
        [
            contract_rows(
                hidden_rim[offset * frame_len : offset * frame_len + tok_local], grad_features
            )
            for offset in range(3)
        ]
    )
    grad_hidden = jnp.zeros((tok_local, channels), jnp.float32)
    for offset in range(3):
        grad_hidden = grad_hidden + jnp.dot(
            grad_rim[(2 - offset) * frame_len : (2 - offset) * frame_len + tok_local],
            w_temporal[offset].T,
            preferred_element_type=jnp.float32,
        )
    grad_pre = (grad_hidden * silu_slope(pre_act)).astype(jnp.bfloat16)
    grad_ws = jnp.stack([contract_rows(taps[offset], grad_pre) for offset in range(9)])
    totals = lax.psum(
        (grad_ws, grad_wt, grad_wq_local, grad_wk_local, grad_wv_local, grad_wo_local),
        ("frame", "dp"),
    )
    factor = float(lax.axis_size("dp") * lax.axis_size("frame") * tok_local) ** (-0.5)
    return (
        totals[0] * factor,
        totals[1] * factor,
        totals[2] * factor,
        totals[3] * factor,
        totals[4] * factor,
        totals[5] * factor,
    )


def solution(mesh):
    in_specs = (
        P("dp", "frame", None),
        P("dp", None),
        P(),
        P(),
        P(None, "head"),
        P(None, "head"),
        P(None, "head"),
        P("head", None),
        P("dp", "frame", None),
    )
    out_specs = (P(), P(), P(None, "head"), P(None, "head"), P(None, "head"), P("head", None))
    return jax.shard_map(
        on_device, mesh=mesh, in_specs=in_specs, out_specs=out_specs, check_vma=False
    )
```

profile of v0, /device:TPU:8, one launch (start us, length us, event | category | flops | bytes accessed | tf_op | source)
XLA Modules:
  0.0 700.0 jit_solution(11616659482293236148)
XLA Ops:
  7.2 1.9 pad_slice_fusion
  13.6 4.0 collective-permute-start
  19.1 4.3 collective-permute-done.1
  24.8 1.7 convolution_convert_fusion
  27.7 85.4 %all-gather.3.cloned.1.call-done = bf16[4096,256]{1,0:T(8,128)(2,1)} async-done(((bf16[256,256]{1,0:T(8,128)(2,1)}), bf16[4096,256]{1,0:T(8,128)(2,1)}) %all-gather.3.cloned.1.call-update) | async-done | bytes 2097168 | tf_op jit(solution)/shard_map/all_gather | solution.py:90
  113.1 2.3 fusion.108
  116.3 1.9 fusion.6
  118.7 2.4 fusion.9
  122.4 1.8 fusion.91
  124.2 1.8 fusion.94
  126.0 72.5 %all-gather.5.cloned.1.call-done = bf16[4096,256]{1,0:T(8,128)(2,1)} async-done(((bf16[256,256]{1,0:T(8,128)(2,1)}), bf16[4096,256]{1,0:T(8,128)(2,1)}) %all-gather.5.cloned.1.call-update) | async-done | bytes 2097168 | tf_op jit(solution)/shard_map/all_gather | solution.py:91
  198.4 2.8 convolution_convert_fusion.5
  201.3 2.9 multiply_reduce_fusion.1
  204.3 1.7 fusion.5
  206.5 1.7 copy-done.4
  208.1 1.7 fusion.4
  213.4 3.8 pad_maximum_fusion
  217.4 2.8 convolution_convert_fusion.6
  223.3 216.4 %reduce-scatter.2.cloned.1.call-done = f32[256,512]{0,1:T(8,128)} async-done(((f32[4096,512]{0,1:T(8,128)}), f32[256,512]{0,1:T(8,128)}) %reduce-scatter.2.cloned.1.call-update) | async-done | bytes 524304 | tf_op jit(solution)/shard_map/reduce_scatter | solution.py:147
  443.9 60.5 %all-reduce.5.cloned.1.call-done = f32[256,256]{1,0:T(8,128)} async-done(((f32[256,256]{1,0:T(8,128)}), f32[256,256]{1,0:T(8,128)}) %all-reduce.5.cloned.1.call-update) | async-done | bytes 262160 | tf_op jit(solution)/shard_map/psum | solution.py:159
  507.1 4.5 collective-permute-start.3
  515.8 1.4 copy-done.9
  517.3 168.9 %all-reduce.7.cloned.1.call-done = (f32[9,256,256]{2,1,0:T(8,128)}, f32[3,256,256]{2,1,0:T(8,128)}, f32[256,256]{1,0:T(8,128)}, f32[256,256]{1,0:T(8,128)}, f32[256,256]{1,0:T(8,128)}, /*index=5*/f32[256,256]{1,0:T(8,128)}) async-done(((f32[9,256,256]{2,1,0:T(8,128)}, f32[3,256,256]{2,1,0:T(8,128)}, f32[256,256]{1,0:T(8,128)}, f32[256,256]{1,0:T(8,128)}, f32[256,256]{1,0:T(8,128)}, ...) | async-done | bytes 4194320 | tf_op jit(solution)/shard_map/psum | solution.py:179
  686.1 3.4 broadcast_multiply_fusion
  (166 shorter events, 32.9 us)
Async XLA Ops:
  7.2 20.4 %copy-start = (bf16[256,256]{1,0:T(8,128)(2,1)S(1)}, bf16[256,256]{1,0:T(8,128)(2,1)}, u32[]{:S(2)}) copy-start(bf16[256,256]{1,0:T(8,128)(2,1)} %param.13) | copy-start | bytes 393220
  7.2 105.9 %all-gather.3.cloned.1.call-start = ((), (), s32[]{:S(2)}) async-start(), calls=%async_computation.1 | async-start | bytes 2228224 | tf_op jit(solution)/shard_map/all_gather | solution.py:90
  12.5 11.3 %copy-start.27 = (bf16[256,256]{1,0:T(8,128)(2,1)S(1)}, bf16[256,256]{1,0:T(8,128)(2,1)}, u32[]{:S(2)}) copy-start(bf16[256,256]{1,0:T(8,128)(2,1)} %param.14) | copy-start | bytes 393220
  12.7 13.9 %copy-start.42 = (s32[1,4096]{1,0:T(1,128)S(1)}, s32[1,4096]{1,0:T(1,128)}, u32[]{:S(2)}) copy-start(s32[1,4096]{1,0:T(1,128)} %param.10) | copy-start | bytes 49156
  12.7 13.9 %copy-start.13 = (bf16[1,256,256]{2,1,0:T(8,128)(2,1)S(1)}, bf16[1,256,256]{2,1,0:T(8,128)(2,1)}, u32[]{:S(2)}) copy-start(bf16[1,256,256]{2,1,0:T(8,128)(2,1)} %param.17) | copy-start | bytes 393220
  13.6 13.0 %copy-start.37 = (bf16[256,256]{1,0:T(8,128)(2,1)S(1)}, bf16[256,256]{1,0:T(8,128)(2,1)}, u32[]{:S(2)}) copy-start(bf16[256,256]{1,0:T(8,128)(2,1)} %param.16) | copy-start | bytes 393220
  13.6 10.0 %collective-permute-start = (bf16[64,256]{1,0:T(8,128)(2,1)S(1)}, bf16[64,256]{1,0:T(8,128)(2,1)S(1)}, u32[]{:S(2)}, u32[]{:S(2)}) collective-permute-start(bf16[64,256]{1,0:T(8,128)(2,1)S(1)} %get-tuple-element.18), channel_id=1, source_target_pairs={{0,16},{16,32},{32,48},{48,64},{64,80},{80,96},{96,112},{112,128},... | collective-permute-start | bytes 98312 | tf_op jit(solution)/shard_map/ppermute | solution.py:19
  17.6 5.8 collective-permute-start.1
  23.4 91.9 %copy-start.38 = (bf16[64,256]{1,0:T(8,128)(2,1)}, bf16[64,256]{1,0:T(8,128)(2,1)S(1)}, u32[]{:S(2)}) copy-start(bf16[64,256]{1,0:T(8,128)(2,1)S(1)} %collective-permute-done.1) | copy-start | bytes 98308
  23.6 91.7 %copy-start.40 = (bf16[64,256]{1,0:T(8,128)(2,1)}, bf16[64,256]{1,0:T(8,128)(2,1)S(1)}, u32[]{:S(2)}) copy-start(bf16[64,256]{1,0:T(8,128)(2,1)S(1)} %collective-permute-done) | copy-start | bytes 98308
  24.7 173.7 %all-gather.5.cloned.1.call-start = ((), (), s32[]{:S(2)}) async-start(), calls=%async_computation.2 | async-start | bytes 2228224 | tf_op jit(solution)/shard_map/all_gather | solution.py:91
  26.5 413.2 %reduce-scatter.2.cloned.1.call-start = ((), (), s32[]{:S(2)}) async-start(), calls=%async_computation.3 | async-start | bytes 8912896 | tf_op jit(solution)/shard_map/reduce_scatter | solution.py:147
  26.6 89.7 %copy-start.43 = (s32[1,256]{1,0:T(1,128)}, s32[1,256]{1,0:T(1,128)S(1)}, u32[]{:S(2)}) copy-start(s32[1,256]{1,0:T(1,128)S(1)} %constant_dynamic-slice_fusion) | copy-start | bytes 3076
  27.7 87.6 %copy-start.25 = (bf16[256,256]{1,0:T(8,128)(2,1)}, bf16[256,256]{1,0:T(8,128)(2,1)S(1)}, u32[]{:S(2)}) copy-start(bf16[256,256]{1,0:T(8,128)(2,1)S(1)} %convolution_convert_fusion.3) | copy-start | bytes 393220
  217.2 287.1 %all-reduce.5.cloned.1.call-start = ((), (), s32[]{:S(2)}) async-start(), calls=%async_computation.4 | async-start | bytes 524288 | tf_op jit(solution)/shard_map/psum | solution.py:159
  221.2 220.5 %copy-start.28 = (bf16[256,256]{1,0:T(8,128)(2,1)S(1)}, bf16[256,256]{1,0:T(8,128)(2,1)}, u32[]{:S(2)}) copy-start(bf16[256,256]{1,0:T(8,128)(2,1)} %param.14) | copy-start | bytes 393220
  221.2 220.8 %copy-start.29 = (bf16[256,256]{1,0:T(8,128)(2,1)S(1)}, bf16[256,256]{1,0:T(8,128)(2,1)}, u32[]{:S(2)}) copy-start(bf16[256,256]{1,0:T(8,128)(2,1)} %param.15) | copy-start | bytes 393220
  223.3 282.3 %copy-start.18 = (bf16[3,256,256]{2,1,0:T(8,128)(2,1)S(1)}, bf16[3,256,256]{2,1,0:T(8,128)(2,1)}, u32[]{:S(2)}) copy-start(bf16[3,256,256]{2,1,0:T(8,128)(2,1)} %param.12) | copy-start | bytes 1179652
  440.8 70.9 %copy-start.41 = (bf16[64,256]{1,0:T(8,128)(2,1)S(1)}, bf16[64,256]{1,0:T(8,128)(2,1)}, u32[]{:S(2)}) copy-start(bf16[64,256]{1,0:T(8,128)(2,1)} %copy-done.40) | copy-start | bytes 98308
  441.7 70.2 %copy-start.39 = (bf16[64,256]{1,0:T(8,128)(2,1)S(1)}, bf16[64,256]{1,0:T(8,128)(2,1)}, u32[]{:S(2)}) copy-start(bf16[64,256]{1,0:T(8,128)(2,1)} %copy-done.38) | copy-start | bytes 98308
  442.9 243.2 %all-reduce.7.cloned.1.call-start = ((), (), s32[]{:S(2)}) async-start(), calls=%async_computation.5 | async-start | bytes 8388608 | tf_op jit(solution)/shard_map/psum | solution.py:179
  443.9 69.6 %copy-start.49 = (f32[256,256]{1,0:T(8,128)S(1)}, f32[256,256]{1,0:T(8,128)}, u32[]{:S(2)}) copy-start(f32[256,256]{1,0:T(8,128)} %get-tuple-element.31) | copy-start | bytes 786436
  505.8 7.7 %collective-permute-start.2 = (bf16[64,256]{1,0:T(8,128)(2,1)S(1)}, bf16[64,256]{1,0:T(8,128)(2,1)S(1)}, u32[]{:S(2)}, u32[]{:S(2)}) collective-permute-start(bf16[64,256]{1,0:T(8,128)(2,1)S(1)} %get-tuple-element.16), channel_id=1, source_target_pairs={{16,0},{32,16},{48,32},{64,48},{80,64},{96,80},{112,96},{128,112},... | collective-permute-start | bytes 98312 | tf_op jit(solution)/shard_map/ppermute | solution.py:21
  507.1 6.1 collective-permute-start.3
  (35 other events, 111.0 us)
Sparse Core Ops, SparseCore 0:
  24.8 88.2 all-gather.2
  116.2 82.1 all-gather.4
  217.3 222.3 reduce-scatter.1
  443.1 61.2 all-reduce.4
  517.4 168.7 all-reduce.6
where the time goes:
time: 700 us
  waiting for transfers between devices  608 us (87%)
  matrix products  37.3 us (5%)
  other arithmetic  18.4 us (3%)
  between operations  14.7 us (2%)
  starting transfers between devices  11.5 us (2%)
  local copies, waits for them, and re-layouts  9.96 us (1%)
    reduce_scatter x1, waiting for transfers between devices, on_device(): lax.psum_scatter(jnp.concatenate(key_parts + value_parts, axis=1), 'frame...  216 us
    psum x1, waiting for transfers between devices, on_device(): lax.psum((grad_ws, grad_wt, grad_wq_local, grad_wk_local, grad_wv_local,...  169 us
    all_gather x1, waiting for transfers between devices, on_device(): lax.all_gather(keys_local, 'frame', axis=0, tiled=True)  85.4 us
    all_gather x1, waiting for transfers between devices, on_device(): lax.all_gather(values_local, 'frame', axis=0, tiled=True)  72.5 us
    psum x1, waiting for transfers between devices, on_device(): head_sum = lax.psum(back_part, 'head')  60.5 us
  transfers between devices with their start and end apart: 9, of which 7 were waited for; matrix products, arithmetic and copies ran while one was open for 3% of the time, Pallas kernels for 0%

commit v1 on v0

--- a/solution.py
+++ b/solution.py
@@ -177,8 +177,10 @@
     grad_pre = (grad_hidden * silu_slope(pre_act)).astype(jnp.bfloat16)
     grad_ws = jnp.stack([contract_rows(taps[offset], grad_pre) for offset in range(9)])
     totals = lax.psum(
-        (grad_ws, grad_wt, grad_wq_local, grad_wk_local, grad_wv_local, grad_wo_local),
-        ("frame", "dp"),
+        lax.psum(
+            (grad_ws, grad_wt, grad_wq_local, grad_wk_local, grad_wv_local, grad_wo_local), "dp"
+        ),
+        "frame",
     )
     factor = float(lax.axis_size("dp") * lax.axis_size("frame") * tok_local) ** (-0.5)
     return (

time: 700 us -> 835 us (1.19)
  waiting for transfers between devices: 608 us -> 743 us
    psum x0 -> x1, waiting for transfers between devices: none -> 178 us  [on_device(): lax.psum(lax.psum((grad_ws, grad_wt, grad_wq_local, grad_wk_local, grad_w...]
    psum x1, waiting for transfers between devices: 169 us -> 125 us  [on_device(): lax.psum((grad_ws, grad_wt, grad_wq_local, grad_wk_local, grad_wv_local,...]
  transfers between devices with their start and end apart: 9 -> 10, of which waited for: 7 -> 8; matrix products, arithmetic and copies ran while one was open for 3% -> 3% of each run, Pallas kernels for 0% -> 0%
where the time goes in v1:
time: 835 us
  waiting for transfers between devices  743 us (89%)
  matrix products  37.3 us (4%)
  other arithmetic  18.4 us (2%)
  between operations  15 us (2%)
  starting transfers between devices  11.5 us (1%)
  local copies, waits for them, and re-layouts  10.2 us (1%)
    reduce_scatter x1, waiting for transfers between devices, on_device(): lax.psum_scatter(jnp.concatenate(key_parts + value_parts, axis=1), 'frame...  217 us
    psum x1, waiting for transfers between devices, on_device(): lax.psum(lax.psum((grad_ws, grad_wt, grad_wq_local, grad_wk_local, grad_w...  178 us
    psum x1, waiting for transfers between devices, on_device(): lax.psum((grad_ws, grad_wt, grad_wq_local, grad_wk_local, grad_wv_local,...  125 us
    all_gather x1, waiting for transfers between devices, on_device(): lax.all_gather(keys_local, 'frame', axis=0, tiled=True)  85.4 us
    all_gather x1, waiting for transfers between devices, on_device(): lax.all_gather(values_local, 'frame', axis=0, tiled=True)  72.5 us
    psum x1, waiting for transfers between devices, on_device(): head_sum = lax.psum(back_part, 'head')  60.3 us
  transfers between devices with their start and end apart: 10, of which 8 were waited for; matrix products, arithmetic and copies ran while one was open for 3% of the time, Pallas kernels for 0%

profile of v1, /device:TPU:8, one launch (start us, length us, event | category | flops | bytes accessed | tf_op | source)
XLA Modules:
  0.0 835.1 jit_solution(9086440338307810512)
XLA Ops:
  7.2 1.7 pad_slice_fusion
  13.4 3.9 collective-permute-start
  18.9 4.3 collective-permute-done.1
  24.9 1.8 convolution_convert_fusion
  27.9 85.4 %all-gather.3.cloned.1.call-done = bf16[4096,256]{1,0:T(8,128)(2,1)} async-done(((bf16[256,256]{1,0:T(8,128)(2,1)}), bf16[4096,256]{1,0:T(8,128)(2,1)}) %all-gather.3.cloned.1.call-update) | async-done | bytes 2097168 | tf_op jit(solution)/shard_map/all_gather | solution.py:90
  113.3 2.3 fusion.108
  116.5 1.9 fusion.6
  118.9 2.4 fusion.9
  122.6 1.7 fusion.91
  124.4 1.8 fusion.94
  126.1 72.5 %all-gather.5.cloned.1.call-done = bf16[4096,256]{1,0:T(8,128)(2,1)} async-done(((bf16[256,256]{1,0:T(8,128)(2,1)}), bf16[4096,256]{1,0:T(8,128)(2,1)}) %all-gather.5.cloned.1.call-update) | async-done | bytes 2097168 | tf_op jit(solution)/shard_map/all_gather | solution.py:91
  198.6 2.8 convolution_convert_fusion.5
  201.5 2.9 multiply_reduce_fusion.1
  204.5 1.7 fusion.5
  206.7 1.7 copy-done.4
  208.3 1.7 fusion.4
  213.6 3.8 pad_maximum_fusion
  217.7 2.8 convolution_convert_fusion.6
  223.5 216.6 %reduce-scatter.2.cloned.1.call-done = f32[256,512]{0,1:T(8,128)} async-done(((f32[4096,512]{0,1:T(8,128)}), f32[256,512]{0,1:T(8,128)}) %reduce-scatter.2.cloned.1.call-update) | async-done | bytes 524304 | tf_op jit(solution)/shard_map/reduce_scatter | solution.py:147
  444.3 60.3 %all-reduce.7.cloned.1.call-done = f32[256,256]{1,0:T(8,128)} async-done(((f32[256,256]{1,0:T(8,128)}), f32[256,256]{1,0:T(8,128)}) %all-reduce.7.cloned.1.call-update) | async-done | bytes 262160 | tf_op jit(solution)/shard_map/psum | solution.py:159
  507.3 4.5 collective-permute-start.3
  517.5 125.2 %all-reduce.11.cloned.1.call-done = (f32[9,256,256]{2,1,0:T(8,128)}, f32[3,256,256]{2,1,0:T(8,128)}, f32[256,256]{1,0:T(8,128)}, f32[256,256]{1,0:T(8,128)}, f32[256,256]{1,0:T(8,128)}, /*index=5*/f32[256,256]{1,0:T(8,128)}) async-done(((f32[9,256,256]{2,1,0:T(8,128)}, f32[3,256,256]{2,1,0:T(8,128)}, f32[256,256]{1,0:T(8,128)}, f32[256,256]{1,0:T(8,128)}, f32[256,256]{1,0:T(8,128)}, ...) | async-done | bytes 4194320 | tf_op jit(solution)/shard_map/psum | solution.py:180
  642.7 178.2 %all-reduce.9.cloned.1.call-done = (f32[9,256,256]{2,1,0:T(8,128)}, f32[3,256,256]{2,1,0:T(8,128)}, f32[256,256]{1,0:T(8,128)}, f32[256,256]{1,0:T(8,128)}, f32[256,256]{1,0:T(8,128)}, /*index=5*/f32[256,256]{1,0:T(8,128)}) async-done(((f32[9,256,256]{2,1,0:T(8,128)}, f32[3,256,256]{2,1,0:T(8,128)}, f32[256,256]{1,0:T(8,128)}, f32[256,256]{1,0:T(8,128)}, f32[256,256]{1,0:T(8,128)}, ...) | async-done | bytes 4194320 | tf_op jit(solution)/shard_map/psum | solution.py:179
  820.9 3.4 broadcast_multiply_fusion
  (169 shorter events, 34.8 us)
Async XLA Ops:
  7.2 20.5 %copy-start = (bf16[256,256]{1,0:T(8,128)(2,1)S(1)}, bf16[256,256]{1,0:T(8,128)(2,1)}, u32[]{:S(2)}) copy-start(bf16[256,256]{1,0:T(8,128)(2,1)} %param.13) | copy-start | bytes 393220
  7.2 106.1 %all-gather.3.cloned.1.call-start = ((), (), s32[]{:S(2)}) async-start(), calls=%async_computation.1 | async-start | bytes 2228224 | tf_op jit(solution)/shard_map/all_gather | solution.py:90
  12.3 11.7 %copy-start.27 = (bf16[256,256]{1,0:T(8,128)(2,1)S(1)}, bf16[256,256]{1,0:T(8,128)(2,1)}, u32[]{:S(2)}) copy-start(bf16[256,256]{1,0:T(8,128)(2,1)} %param.14) | copy-start | bytes 393220
  12.5 14.3 %copy-start.42 = (s32[1,4096]{1,0:T(1,128)S(1)}, s32[1,4096]{1,0:T(1,128)}, u32[]{:S(2)}) copy-start(s32[1,4096]{1,0:T(1,128)} %param.10) | copy-start | bytes 49156
  12.5 14.3 %copy-start.13 = (bf16[1,256,256]{2,1,0:T(8,128)(2,1)S(1)}, bf16[1,256,256]{2,1,0:T(8,128)(2,1)}, u32[]{:S(2)}) copy-start(bf16[1,256,256]{2,1,0:T(8,128)(2,1)} %param.17) | copy-start | bytes 393220
  13.4 13.4 %copy-start.37 = (bf16[256,256]{1,0:T(8,128)(2,1)S(1)}, bf16[256,256]{1,0:T(8,128)(2,1)}, u32[]{:S(2)}) copy-start(bf16[256,256]{1,0:T(8,128)(2,1)} %param.16) | copy-start | bytes 393220
  13.4 10.4 %collective-permute-start = (bf16[64,256]{1,0:T(8,128)(2,1)S(1)}, bf16[64,256]{1,0:T(8,128)(2,1)S(1)}, u32[]{:S(2)}, u32[]{:S(2)}) collective-permute-start(bf16[64,256]{1,0:T(8,128)(2,1)S(1)} %get-tuple-element.24), channel_id=1, source_target_pairs={{0,16},{16,32},{32,48},{48,64},{64,80},{80,96},{96,112},{112,128},... | collective-permute-start | bytes 98312 | tf_op jit(solution)/shard_map/ppermute | solution.py:19
  17.4 5.8 collective-permute-start.1
  23.8 91.7 %copy-start.40 = (bf16[64,256]{1,0:T(8,128)(2,1)}, bf16[64,256]{1,0:T(8,128)(2,1)S(1)}, u32[]{:S(2)}) copy-start(bf16[64,256]{1,0:T(8,128)(2,1)S(1)} %collective-permute-done) | copy-start | bytes 98308
  24.9 173.7 %all-gather.5.cloned.1.call-start = ((), (), s32[]{:S(2)}) async-start(), calls=%async_computation.2 | async-start | bytes 2228224 | tf_op jit(solution)/shard_map/all_gather | solution.py:91
  26.7 413.3 %reduce-scatter.2.cloned.1.call-start = ((), (), s32[]{:S(2)}) async-start(), calls=%async_computation.3 | async-start | bytes 8912896 | tf_op jit(solution)/shard_map/reduce_scatter | solution.py:147
  26.8 89.7 %copy-start.43 = (s32[1,256]{1,0:T(1,128)}, s32[1,256]{1,0:T(1,128)S(1)}, u32[]{:S(2)}) copy-start(s32[1,256]{1,0:T(1,128)S(1)} %constant_dynamic-slice_fusion) | copy-start | bytes 3076
  27.9 87.7 %copy-start.25 = (bf16[256,256]{1,0:T(8,128)(2,1)}, bf16[256,256]{1,0:T(8,128)(2,1)S(1)}, u32[]{:S(2)}) copy-start(bf16[256,256]{1,0:T(8,128)(2,1)S(1)} %convolution_convert_fusion.3) | copy-start | bytes 393220
  217.4 287.1 %all-reduce.7.cloned.1.call-start = ((), (), s32[]{:S(2)}) async-start(), calls=%async_computation.4 | async-start | bytes 524288 | tf_op jit(solution)/shard_map/psum | solution.py:159
  221.4 220.7 %copy-start.28 = (bf16[256,256]{1,0:T(8,128)(2,1)S(1)}, bf16[256,256]{1,0:T(8,128)(2,1)}, u32[]{:S(2)}) copy-start(bf16[256,256]{1,0:T(8,128)(2,1)} %param.14) | copy-start | bytes 393220
  221.4 220.9 %copy-start.29 = (bf16[256,256]{1,0:T(8,128)(2,1)S(1)}, bf16[256,256]{1,0:T(8,128)(2,1)}, u32[]{:S(2)}) copy-start(bf16[256,256]{1,0:T(8,128)(2,1)} %param.15) | copy-start | bytes 393220
  223.5 282.3 %copy-start.18 = (bf16[3,256,256]{2,1,0:T(8,128)(2,1)S(1)}, bf16[3,256,256]{2,1,0:T(8,128)(2,1)}, u32[]{:S(2)}) copy-start(bf16[3,256,256]{2,1,0:T(8,128)(2,1)} %param.12) | copy-start | bytes 1179652
  441.1 70.7 %copy-start.41 = (bf16[64,256]{1,0:T(8,128)(2,1)S(1)}, bf16[64,256]{1,0:T(8,128)(2,1)}, u32[]{:S(2)}) copy-start(bf16[64,256]{1,0:T(8,128)(2,1)} %copy-done.40) | copy-start | bytes 98308
  442.1 70.0 %copy-start.39 = (bf16[64,256]{1,0:T(8,128)(2,1)S(1)}, bf16[64,256]{1,0:T(8,128)(2,1)}, u32[]{:S(2)}) copy-start(bf16[64,256]{1,0:T(8,128)(2,1)} %copy-done.38) | copy-start | bytes 98308
  443.3 199.4 %all-reduce.11.cloned.1.call-start = ((), (), s32[]{:S(2)}) async-start(), calls=%async_computation.6 | async-start | bytes 8388608 | tf_op jit(solution)/shard_map/psum | solution.py:180
  444.3 69.4 %copy-start.49 = (f32[256,256]{1,0:T(8,128)S(1)}, f32[256,256]{1,0:T(8,128)}, u32[]{:S(2)}) copy-start(f32[256,256]{1,0:T(8,128)} %get-tuple-element.37) | copy-start | bytes 786436
  506.0 7.7 collective-permute-start.2
  507.3 6.1 collective-permute-start.3
  517.5 303.5 %all-reduce.9.cloned.1.call-start = ((), (), s32[]{:S(2)}) async-start(), calls=%async_computation.5 | async-start | bytes 8388608 | tf_op jit(solution)/shard_map/psum | solution.py:179
  (36 other events, 111.3 us)
Sparse Core Ops, SparseCore 0:
  25.0 88.2 all-gather.2
  116.4 82.1 all-gather.4
  217.5 222.4 reduce-scatter.1
  443.4 61.0 all-reduce.6
  517.6 125.0 all-reduce.10
  645.6 175.2 all-reduce.8
